TPU v7x, 32 devices: a whole 2x2x4 slice. The times are simulated.
32 devices in a mesh: member: 8 (over y, x, core), region: 4 (over z).
Axes of the slice: x: 2, y: 2, z: 4, core: 2. Of those that a mesh axis runs over, the one named last changes fastest.
Arguments:
- state: float32 [256, 8, 4096], P('member', None, 'region'), may hold values from -6 to 6
- adjacent_columns: int32 [6, 4096], P(None, 'region'), may hold values from 0 to 4095, as said below
- adjacent_rates: float32 [6, 4096], P(None, 'region'), may hold values from 0.02 to 0.16
- amplification_speed: float32 [4096], P('region'), may hold values from 0.05 to 0.5
- obs_patch: int32 [8192], P(('member', 'region')), may hold values from -1 to 31, as said below
- obs_row: int32 [8192], P(('member', 'region')), may hold values from 0 to 1023
- obs_value: float32 [8192], P(('member', 'region')), may hold values from -6 to 6
- obs_error: float32 [8192], P(('member', 'region')), may hold values from 0.5 to 2
Outputs:
- analysis: bfloat16 [256, 8, 4096], P('member', None, 'region')
Inputs may be any that keep to these rules, and one draw needn't show every extreme that they name: `adjacent_columns`: each neighbour lies within 256 positions of its column along the closed order of columns (index modulo 4096) and is never the column itself. `obs_patch`: at most 256 rows name one patch. Within the 256 rows of one device, at most 8 rows name any one patch; -1 marks a row without an observation.
All inputs are finite; a program needn't handle non-finite values.
Results may differ from a plain program's by a relative error of at most 0.01.
Values may be sent and summed in bfloat16 or wider, within the bound.
A program may use at most 64 MiB of HBM per device.

v0:
```python
import math

import jax
import jax.numpy as jnp
from jax import lax
from jax.sharding import PartitionSpec as P

PATCH_CELLS = 128
PATCH_DEV = 1
PATCH_OBS = 256
RIM = 256
STEPS = 3
NS_ITERS = 6


def padded_2(value, sides, width):
    for axis, dim in sides:
        size, length = (lax.axis_size(axis), value.shape[dim])
        up = [(i, (i + 1) % size) for i in range(size)]
        down = [(j, i) for i, j in up]
        last = lax.slice_in_dim(value, length - width, length, axis=dim)
        first = lax.slice_in_dim(value, 0, width, axis=dim)
        before = lax.ppermute(last, axis, up)
        after = lax.ppermute(first, axis, down)
        value = jnp.concatenate([before, value, after], axis=dim)
    return value


def advance(padded, adjacent_rates, amplification_speed, offsets):
    length = offsets.shape[1]
    width = (padded.shape[2] - length) // 2
    members = padded.shape[0]
    level_values = padded.shape[1]
    flat = padded.reshape(members * level_values, padded.shape[2])
    block = math.gcd(length, 128)
    count_blocks = length // block
    window_len = block + 2 * RIM
    source = jnp.arange(window_len, dtype=jnp.int32)[:, None]
    column = jnp.arange(block, dtype=jnp.int32)[None, :]

    def one_block(index):
        first = index * block
        window = lax.dynamic_slice_in_dim(flat, first + width - RIM, window_len, 1)
        centre = lax.dynamic_slice_in_dim(flat, first + width, block, 1)
        rate_block = lax.dynamic_slice_in_dim(adjacent_rates, first, block, 1)
        offset_block = lax.dynamic_slice_in_dim(offsets, first, block, 1)
        speed_block = lax.dynamic_slice_in_dim(amplification_speed, first, block, 0)
        local = offset_block + RIM + column
        matrix = jnp.zeros((window_len, block), jnp.float32)
        for neighbour in range(6):
            matrix = matrix + jnp.where(
                source == local[neighbour][None, :], rate_block[neighbour][None, :], 0.0
            )
        summed = (
            jnp.dot(window, matrix, precision=lax.Precision.HIGHEST)
            - centre * jnp.sum(rate_block, axis=0)[None, :]
        )
        blended = centre + summed
        return blended + speed_block[None, :] * jnp.tanh(blended)

    produced = lax.map(one_block, jnp.arange(count_blocks, dtype=jnp.int32))
    return produced.transpose(1, 0, 2).reshape(members, level_values, length)


def running_rank(onehot):
    rows = onehot.shape[0]
    lower = (
        jnp.arange(rows, dtype=jnp.int32)[:, None] >= jnp.arange(rows, dtype=jnp.int32)[None, :]
    ).astype(jnp.bfloat16)
    counts = jnp.dot(lower, onehot.astype(jnp.bfloat16), preferred_element_type=jnp.float32)
    return (jnp.sum(counts * onehot, axis=1) - 1.0).astype(jnp.int32)


def analyse(ensemble_realizations, row_index, values, weight_matrix):
    ensemble = ensemble_realizations.shape[0]
    span = ensemble_realizations.shape[1]
    average = jnp.mean(ensemble_realizations, axis=0)
    anomaly = ensemble_realizations - average[None, :]
    select = (jnp.arange(span, dtype=jnp.int32)[:, None] == row_index[None, :]).astype(jnp.float32)
    observed = jnp.dot(anomaly, select, precision=lax.Precision.HIGHEST)
    innovation = values - jnp.dot(average, select, precision=lax.Precision.HIGHEST)
    rooted = jnp.sqrt(weight_matrix)
    spread = math.sqrt(ensemble - 1.0)
    scaled = observed * rooted[None, :] / spread
    identity = jnp.eye(ensemble, dtype=jnp.float32)
    system = identity + jnp.dot(scaled, scaled.T, precision=lax.Precision.HIGHEST)
    norm_fro = jnp.sqrt(jnp.sum(system * system))
    iterate = system / norm_fro
    inverse_root = identity
    for sweep in range(NS_ITERS):
        factor = 1.5 * identity - 0.5 * jnp.dot(
            inverse_root, iterate, precision=lax.Precision.HIGHEST
        )
        iterate = jnp.dot(iterate, factor, precision=lax.Precision.HIGHEST)
        inverse_root = jnp.dot(factor, inverse_root, precision=lax.Precision.HIGHEST)
    forcing_term = jnp.dot(scaled, rooted * innovation, precision=lax.Precision.HIGHEST) / spread
    inner_shift = jnp.dot(inverse_root, forcing_term, precision=lax.Precision.HIGHEST)
    mean_shift = jnp.dot(inverse_root, inner_shift, precision=lax.Precision.HIGHEST) / norm_fro
    transform = inverse_root / jnp.sqrt(norm_fro) + mean_shift[:, None]
    updated = average[None, :] + jnp.dot(transform.T, anomaly, precision=lax.Precision.HIGHEST)
    return updated.astype(jnp.bfloat16)


def on_device(
    state,
    adjacent_columns,
    adjacent_rates,
    amplification_speed,
    obs_patch,
    obs_row,
    obs_value,
    obs_error,
):
    level_values = state.shape[1]
    cell_dev = state.shape[2]
    regions = lax.axis_size("region")
    groups = lax.axis_size("member")
    cells_all = cell_dev * regions
    cell_index = lax.axis_index("region") * cell_dev + jnp.arange(cell_dev, dtype=jnp.int32)
    offsets = (adjacent_columns - cell_index[None, :] + cells_all // 2) % cells_all - cells_all // 2
    model_variable_array = state
    for section_index in range(STEPS):
        padded = padded_2(model_variable_array, (("region", 2),), RIM)
        model_variable_array = advance(padded, adjacent_rates, amplification_speed, offsets)
    rounded = model_variable_array.astype(jnp.bfloat16)
    patched = lax.all_to_all(rounded, "member", split_axis=2, concat_axis=0, tiled=True)
    devices = groups * regions
    slots = obs_patch.shape[0] // devices
    is_live = obs_patch >= 0
    patch_id = jnp.maximum(obs_patch, 0)
    per_region = groups * PATCH_DEV
    target = jnp.where(
        is_live, patch_id % per_region // PATCH_DEV * regions + patch_id // per_region, devices
    )
    onehot = (target[:, None] == jnp.arange(devices, dtype=jnp.int32)[None, :]).astype(jnp.float32)
    ranking = running_rank(onehot)
    spot = jnp.where(is_live, target * slots + ranking, devices * slots)
    span = level_values * PATCH_CELLS
    location_plus = jnp.where(is_live, patch_id % PATCH_DEV * span + obs_row + 1, 0).astype(
        jnp.float32
    )
    weight = jnp.where(is_live, 1.0 / (obs_error * obs_error), 0.0)
    reading = jnp.where(is_live, obs_value, 0.0)
    payload = jnp.stack([location_plus, reading, weight])
    place_hot = (spot[:, None] == jnp.arange(devices * slots, dtype=jnp.int32)[None, :]).astype(
        jnp.float32
    )
    message_bundle = jnp.dot(payload, place_hot, precision=lax.Precision.HIGHEST)
    message_bundle = message_bundle - jnp.array([1.0, 0.0, 0.0], jnp.float32)[:, None]
    arrived = lax.all_to_all(
        message_bundle, ("member", "region"), split_axis=1, concat_axis=1, tiled=True
    )
    received = arrived[0].astype(jnp.int32)
    got_live = received >= 0
    owner = jnp.where(got_live, received // span, PATCH_DEV)
    owner_hot = (owner[:, None] == jnp.arange(PATCH_DEV, dtype=jnp.int32)[None, :]).astype(
        jnp.float32
    )
    owner_rank = running_rank(owner_hot)
    grid_spot = jnp.where(got_live, owner * PATCH_OBS + owner_rank, PATCH_DEV * PATCH_OBS)
    grid_hot = (
        grid_spot[:, None] == jnp.arange(PATCH_DEV * PATCH_OBS, dtype=jnp.int32)[None, :]
    ).astype(jnp.float32)
    position = jnp.where(got_live, received % span, 0).astype(jnp.float32)
    filled = jnp.dot(
        jnp.stack([position, arrived[1], arrived[2]]), grid_hot, precision=lax.Precision.HIGHEST
    )
    row_grid = filled[0].astype(jnp.int32).reshape(PATCH_DEV, PATCH_OBS)
    value_grid = filled[1].reshape(PATCH_DEV, PATCH_OBS)
    analysis_coefficient_array = filled[2].reshape(PATCH_DEV, PATCH_OBS)
    members_all = patched.shape[0]
    blocks = patched.astype(jnp.float32).reshape(members_all, level_values, PATCH_DEV, PATCH_CELLS)
    blocks = blocks.transpose(2, 0, 1, 3).reshape(PATCH_DEV, members_all, span)
    analysed = jax.vmap(analyse)(blocks, row_grid, value_grid, analysis_coefficient_array)
    returned = analysed.reshape(PATCH_DEV, members_all, level_values, PATCH_CELLS).transpose(
        1, 2, 0, 3
    )
    returned = returned.reshape(members_all, level_values, PATCH_DEV * PATCH_CELLS)
    return lax.all_to_all(returned, "member", split_axis=0, concat_axis=2, tiled=True)


def solution(mesh):
    return jax.shard_map(
        on_device,
        mesh=mesh,
        in_specs=(
            P("member", None, "region"),
            P(None, "region"),
            P(None, "region"),
            P("region"),
            P(("member", "region")),
            P(("member", "region")),
            P(("member", "region")),
            P(("member", "region")),
        ),
        out_specs=P("member", None, "region"),
        check_vma=False,
    )
```

profile of v0, /device:TPU:0, one launch (start us, length us, event | category | flops | bytes accessed | tf_op | source)
XLA Modules:
  0.0 186.9 jit_solution(15793519141338912558)
XLA Ops:
  0.0 1.2 fusion.167
  1.2 3.1 %collective-permute-start = (f32[32,8,256]{2,1,0:T(8,128)S(1)}, f32[32,8,256]{2,1,0:T(8,128)S(1)}, u32[]{:S(2)}, u32[]{:S(2)}) collective-permute-start(f32[32,8,256]{2,1,0:T(8,128)S(1)} %get-tuple-element.812), channel_id=1, source_target_pairs={{0,1},{1,2},{2,3},{3,0},{4,5},{5,6},{6,7},{7,4},{8,9},{9,10},{10,1... | collective-permute-start | bytes 786440 | tf_op jit(solution)/shard_map/ppermute | solution.py:23
  4.3 2.1 %collective-permute-start.1 = (f32[32,8,256]{2,1,0:T(8,128)S(1)}, f32[32,8,256]{2,1,0:T(8,128)S(1)}, u32[]{:S(2)}, u32[]{:S(2)}) collective-permute-start(f32[32,8,256]{2,1,0:T(8,128)S(1)} %get-tuple-element.813), channel_id=1, source_target_pairs={{1,0},{2,1},{3,2},{0,3},{5,4},{6,5},{7,6},{4,7},{9,8},{10,9},{11,1... | collective-permute-start | bytes 786440 | tf_op jit(solution)/shard_map/ppermute | solution.py:24
  10.4 4.2 %all-to-all-start.1 = ((f32[3,32,8]{2,0,1:T(4,128)}), f32[3,32,8]{2,0,1:T(4,128)S(1)}, u32[]{:S(2)}, u32[]{:S(2)}) async-start(f32[3,32,8]{2,0,1:T(4,128)} %copy.60), calls=%async_computation.1 | async-start | bytes 131072 | tf_op jit(solution)/shard_map/all_to_all | solution.py:150
  15.5 6.6 %all-to-all-done.1 = f32[3,32,8]{2,0,1:T(4,128)S(1)} async-done(((f32[3,32,8]{2,0,1:T(4,128)}), f32[3,32,8]{2,0,1:T(4,128)S(1)}, u32[]{:S(2)}, u32[]{:S(2)}) %all-to-all-start.1) | async-done | bytes 3104 | tf_op jit(solution)/shard_map/all_to_all | solution.py:150
  22.8 28.6 %while.48 = (s32[]{:T(128)}, f32[8,256,128]{2,1,0:T(8,128)S(1)}, s32[8]{0:T(128)S(1)}, f32[256,1536]{1,0:T(8,128)S(1)}, s32[6,1024]{1,0:T(8,128)S(1)}, /*index=5...) while((s32[]{:T(128)}, f32[8,256,128]{2,1,0:T(8,128)S(1)}, ...), condition=%wide.region_2.3_spmd.clone.clone, body=%wide.region_0.2_spmd.clone.clone.sunk | while | flops 253216912 | bytes 951070 | solution.py:61
  25.5 0.9 bitcast_dynamic-update-slice_fusion.6
  29.1 0.9 bitcast_dynamic-update-slice_fusion.6
  32.7 0.9 bitcast_dynamic-update-slice_fusion.6
  36.2 0.9 bitcast_dynamic-update-slice_fusion.6
  39.8 0.9 bitcast_dynamic-update-slice_fusion.6
  43.4 0.9 bitcast_dynamic-update-slice_fusion.6
  47.0 0.9 bitcast_dynamic-update-slice_fusion.6
  50.6 0.9 bitcast_dynamic-update-slice_fusion.6
  52.6 3.6 %collective-permute-start.3 = (f32[32,8,256]{2,1,0:T(8,128)S(1)}, f32[32,8,256]{2,1,0:T(8,128)S(1)}, u32[]{:S(2)}, u32[]{:S(2)}) collective-permute-start(f32[32,8,256]{2,1,0:T(8,128)S(1)} %get-tuple-element.811), channel_id=1, source_target_pairs={{1,0},{2,1},{3,2},{0,3},{5,4},{6,5},{7,6},{4,7},{9,8},{10,9},{11,1... | collective-permute-start | bytes 786440 | tf_op jit(solution)/shard_map/ppermute | solution.py:24
  56.3 7.0 %collective-permute-done.2 = f32[32,8,256]{2,1,0:T(8,128)S(1)} collective-permute-done((f32[32,8,256]{2,1,0:T(8,128)S(1)}, f32[32,8,256]{2,1,0:T(8,128)S(1)}, u32[]{:S(2)}, u32[]{:S(2)}) %collective-permute-start.2) | collective-permute-done | bytes 262176 | tf_op jit(solution)/shard_map/ppermute | solution.py:23
  63.3 2.9 %collective-permute-done.3 = f32[32,8,256]{2,1,0:T(8,128)S(1)} collective-permute-done((f32[32,8,256]{2,1,0:T(8,128)S(1)}, f32[32,8,256]{2,1,0:T(8,128)S(1)}, u32[]{:S(2)}, u32[]{:S(2)}) %collective-permute-start.3) | collective-permute-done | bytes 262176 | tf_op jit(solution)/shard_map/ppermute | solution.py:24
  66.5 28.6 %while.49 = (s32[]{:T(128)}, f32[8,256,128]{2,1,0:T(8,128)S(1)}, s32[8]{0:T(128)S(1)}, f32[256,1536]{1,0:T(8,128)S(1)}, s32[6,1024]{1,0:T(8,128)S(1)}, /*index=5...) while((s32[]{:T(128)}, f32[8,256,128]{2,1,0:T(8,128)S(1)}, ...), condition=%wide.region_5.6_spmd.clone.clone, body=%wide.region_3.5_spmd.clone.clone.sunk | while | flops 253216912 | bytes 951070 | solution.py:61
  69.2 0.9 bitcast_dynamic-update-slice_fusion.7
  72.7 0.9 bitcast_dynamic-update-slice_fusion.7
  76.3 0.9 bitcast_dynamic-update-slice_fusion.7
  79.9 0.9 bitcast_dynamic-update-slice_fusion.7
  83.5 0.9 bitcast_dynamic-update-slice_fusion.7
  87.1 0.9 bitcast_dynamic-update-slice_fusion.7
  90.7 0.9 bitcast_dynamic-update-slice_fusion.7
  94.2 0.9 bitcast_dynamic-update-slice_fusion.7
  96.5 3.4 %collective-permute-start.5 = (f32[32,8,256]{2,1,0:T(8,128)S(1)}, f32[32,8,256]{2,1,0:T(8,128)S(1)}, u32[]{:S(2)}, u32[]{:S(2)}) collective-permute-start(f32[32,8,256]{2,1,0:T(8,128)S(1)} %get-tuple-element.809), channel_id=1, source_target_pairs={{1,0},{2,1},{3,2},{0,3},{5,4},{6,5},{7,6},{4,7},{9,8},{10,9},{11,1... | collective-permute-start | bytes 786440 | tf_op jit(solution)/shard_map/ppermute | solution.py:24
  100.0 7.0 %collective-permute-done.4 = f32[32,8,256]{2,1,0:T(8,128)S(1)} collective-permute-done((f32[32,8,256]{2,1,0:T(8,128)S(1)}, f32[32,8,256]{2,1,0:T(8,128)S(1)}, u32[]{:S(2)}, u32[]{:S(2)}) %collective-permute-start.4) | collective-permute-done | bytes 262176 | tf_op jit(solution)/shard_map/ppermute | solution.py:23
  107.0 2.1 %collective-permute-done.5 = f32[32,8,256]{2,1,0:T(8,128)S(1)} collective-permute-done((f32[32,8,256]{2,1,0:T(8,128)S(1)}, f32[32,8,256]{2,1,0:T(8,128)S(1)}, u32[]{:S(2)}, u32[]{:S(2)}) %collective-permute-start.5) | collective-permute-done | bytes 262176 | tf_op jit(solution)/shard_map/ppermute | solution.py:24
  110.2 29.4 %while.50 = (s32[]{:T(128)}, bf16[8,256,128]{2,1,0:T(8,128)(2,1)S(1)}, s32[8]{0:T(128)S(1)}, f32[256,1536]{1,0:T(8,128)S(1)}, s32[6,1024]{1,0:T(8,128)S(1)}, /*i...) while((s32[]{:T(128)}, ...), condition=%wide.region_8.9_spmd.clone.clone, body=%wide.region_6.8_spmd.clone.clone.sunk | while | flops 253216912 | bytes 951070 | solution.py:61
  112.9 0.9 bitcast_dynamic-update-slice_fusion.8
  116.6 0.9 bitcast_dynamic-update-slice_fusion.8
  120.3 0.9 bitcast_dynamic-update-slice_fusion.8
  123.9 0.9 bitcast_dynamic-update-slice_fusion.8
  127.6 0.9 bitcast_dynamic-update-slice_fusion.8
  131.3 0.9 bitcast_dynamic-update-slice_fusion.8
  135.0 0.9 bitcast_dynamic-update-slice_fusion.8
  138.7 0.9 bitcast_dynamic-update-slice_fusion.8
  140.2 1.8 copy.57
  142.0 2.7 %reshape.470 = bf16[8,2,16384]{2,1,0:T(2,128)(2,1)} reshape(bf16[1024,8,32]{2,1,0:T(8,128)(2,1)S(1)} %bitcast.232) | data formatting | bytes 1048576
  144.6 3.5 %all-to-all-start = ((bf16[8,2,16384]{2,1,0:T(2,128)(2,1)}), bf16[8,2,16384]{2,1,0:T(2,128)(2,1)S(1)}, u32[]{:S(2)}, u32[]{:S(2)}) async-start(bf16[8,2,16384]{2,1,0:T(2,128)(2,1)} %reshape.470), calls=%async_computation | async-start | bytes 1048576 | tf_op jit(solution)/shard_map/all_to_all | solution.py:126
  148.6 9.2 %all-to-all-done = bf16[8,2,16384]{2,1,0:T(2,128)(2,1)S(1)} async-done(((bf16[8,2,16384]{2,1,0:T(2,128)(2,1)}), bf16[8,2,16384]{2,1,0:T(2,128)(2,1)S(1)}, u32[]{:S(2)}, u32[]{:S(2)}) %all-to-all-start) | async-done | bytes 524320 | tf_op jit(solution)/shard_map/all_to_all | solution.py:126
  157.8 1.0 reshape.471
  158.8 2.1 %copy.58 = bf16[32,8,1024]{2,1,0:T(8,128)(2,1)S(1)} copy(bf16[32,8,1024]{0,1,2:T(8,128)(2,1)S(1)} %bitcast.233) | data formatting | bytes 1048576 | tf_op jit(solution)/shard_map/all_to_all | solution.py:126
  162.5 1.0 multiply_reduce_fusion
  172.5 1.2 fusion.109
  173.8 12.1 %all_to_all.36 = bf16[256,8,128]{2,1,0:T(8,128)(2,1)S(1)} all-to-all(bf16[256,8,128]{2,1,0:T(8,128)(2,1)S(1)} %bitcast.237), channel_id=1, replica_groups=mesh['member'=8,'region'=4] {'member'}, dimensions={0} | all-to-all | bytes 1048576 | tf_op jit(solution)/shard_map/all_to_all | solution.py:179
  185.9 0.9 copy.87
  (228 shorter events, 70.1 us)
Async XLA Ops:
  0.0 22.6 %copy-start = (f32[32,8,1024]{2,1,0:T(8,128)S(1)}, f32[32,8,1024]{2,1,0:T(8,128)}, u32[]{:S(2)}) copy-start(f32[32,8,1024]{2,1,0:T(8,128)} %param.15) | copy-start | bytes 3145732
  0.0 14.6 %copy-start.2 = (s32[6,1024]{1,0:T(8,128)S(1)}, s32[6,1024]{1,0:T(8,128)}, u32[]{:S(2)}) copy-start(s32[6,1024]{1,0:T(8,128)} %param.16) | copy-start | bytes 73732
  1.2 21.4 %collective-permute-start = (f32[32,8,256]{2,1,0:T(8,128)S(1)}, f32[32,8,256]{2,1,0:T(8,128)S(1)}, u32[]{:S(2)}, u32[]{:S(2)}) collective-permute-start(f32[32,8,256]{2,1,0:T(8,128)S(1)} %get-tuple-element.812), channel_id=1, source_target_pairs={{0,1},{1,2},{2,3},{3,0},{4,5},{5,6},{6,7},{7,4},{8,9},{9,10},{10,1... | collective-permute-start | bytes 786440 | tf_op jit(solution)/shard_map/ppermute | solution.py:23
  4.3 18.3 %collective-permute-start.1 = (f32[32,8,256]{2,1,0:T(8,128)S(1)}, f32[32,8,256]{2,1,0:T(8,128)S(1)}, u32[]{:S(2)}, u32[]{:S(2)}) collective-permute-start(f32[32,8,256]{2,1,0:T(8,128)S(1)} %get-tuple-element.813), channel_id=1, source_target_pairs={{1,0},{2,1},{3,2},{0,3},{5,4},{6,5},{7,6},{4,7},{9,8},{10,9},{11,1... | collective-permute-start | bytes 786440 | tf_op jit(solution)/shard_map/ppermute | solution.py:24
  10.4 11.7 %all-to-all-start.1 = ((f32[3,32,8]{2,0,1:T(4,128)}), f32[3,32,8]{2,0,1:T(4,128)S(1)}, u32[]{:S(2)}, u32[]{:S(2)}) async-start(f32[3,32,8]{2,0,1:T(4,128)} %copy.60), calls=%async_computation.1 | async-start | bytes 131072 | tf_op jit(solution)/shard_map/all_to_all | solution.py:150
  52.3 11.0 %collective-permute-start.2 = (f32[32,8,256]{2,1,0:T(8,128)S(1)}, f32[32,8,256]{2,1,0:T(8,128)S(1)}, u32[]{:S(2)}, u32[]{:S(2)}) collective-permute-start(f32[32,8,256]{2,1,0:T(8,128)S(1)} %get-tuple-element.810), channel_id=1, source_target_pairs={{0,1},{1,2},{2,3},{3,0},{4,5},{5,6},{6,7},{7,4},{8,9},{9,10},{10,1... | collective-permute-start | bytes 786440 | tf_op jit(solution)/shard_map/ppermute | solution.py:23
  52.6 13.7 %collective-permute-start.3 = (f32[32,8,256]{2,1,0:T(8,128)S(1)}, f32[32,8,256]{2,1,0:T(8,128)S(1)}, u32[]{:S(2)}, u32[]{:S(2)}) collective-permute-start(f32[32,8,256]{2,1,0:T(8,128)S(1)} %get-tuple-element.811), channel_id=1, source_target_pairs={{1,0},{2,1},{3,2},{0,3},{5,4},{6,5},{7,6},{4,7},{9,8},{10,9},{11,1... | collective-permute-start | bytes 786440 | tf_op jit(solution)/shard_map/ppermute | solution.py:24
  96.0 11.0 %collective-permute-start.4 = (f32[32,8,256]{2,1,0:T(8,128)S(1)}, f32[32,8,256]{2,1,0:T(8,128)S(1)}, u32[]{:S(2)}, u32[]{:S(2)}) collective-permute-start(f32[32,8,256]{2,1,0:T(8,128)S(1)} %get-tuple-element.808), channel_id=1, source_target_pairs={{0,1},{1,2},{2,3},{3,0},{4,5},{5,6},{6,7},{7,4},{8,9},{9,10},{10,1... | collective-permute-start | bytes 786440 | tf_op jit(solution)/shard_map/ppermute | solution.py:23
  96.5 12.6 %collective-permute-start.5 = (f32[32,8,256]{2,1,0:T(8,128)S(1)}, f32[32,8,256]{2,1,0:T(8,128)S(1)}, u32[]{:S(2)}, u32[]{:S(2)}) collective-permute-start(f32[32,8,256]{2,1,0:T(8,128)S(1)} %get-tuple-element.809), channel_id=1, source_target_pairs={{1,0},{2,1},{3,2},{0,3},{5,4},{6,5},{7,6},{4,7},{9,8},{10,9},{11,1... | collective-permute-start | bytes 786440 | tf_op jit(solution)/shard_map/ppermute | solution.py:24
  109.1 1.0 copy-start.1
  144.6 13.2 %all-to-all-start = ((bf16[8,2,16384]{2,1,0:T(2,128)(2,1)}), bf16[8,2,16384]{2,1,0:T(2,128)(2,1)S(1)}, u32[]{:S(2)}, u32[]{:S(2)}) async-start(bf16[8,2,16384]{2,1,0:T(2,128)(2,1)} %reshape.470), calls=%async_computation | async-start | bytes 1048576 | tf_op jit(solution)/shard_map/all_to_all | solution.py:126
where the time goes:
time: 190 us; the launch traced here: 187 us
  local copies, waits for them, and re-layouts  47.8 us (25%)
  waiting for transfers between devices  34.9 us (18%)
  matrix products  33.5 us (18%)
  other arithmetic  21.3 us (11%)
  starting transfers between devices  20.7 us (11%)
  loops' own time  15.3 us (8%)
  blocking collectives  12.1 us (6%)
    dot_general x24, matrix products, one_block(): jnp.dot(window, matrix, precision=lax.Precision.HIGHEST)  21.4 us
    dynamic_slice x24, local copies, waits for them, and re-layouts, one_block(): speed_block = lax.dynamic_slice_in_dim(amplification_speed, first, block, 0)  18.4 us
    reduce_sum x24, other arithmetic, one_block(): jnp.sum(rate_block, axis=0)[None, :]  17 us
    another operation x3, loops' own time, advance(): produced = lax.map(one_block, jnp.arange(count_blocks, dtype=jnp.int32))  15.3 us
    dynamic_slice x24, local copies, waits for them, and re-layouts, advance(): produced = lax.map(one_block, jnp.arange(count_blocks, dtype=jnp.int32))  14.1 us
    ppermute x3, waiting for transfers between devices, padded_2(): before = lax.ppermute(last, axis, up)  14.1 us
    all_to_all x1, blocking collectives, on_device(): lax.all_to_all(returned, 'member', split_axis=0, concat_axis=2, tiled=True)  12.1 us
    all_to_all x1, waiting for transfers between devices, on_device(): lax.all_to_all(rounded, 'member', split_axis=2, concat_axis=0, tiled=True)  9.22 us
  transfers between devices with their start and end apart: 8, of which 6 were waited for; matrix products, arithmetic and copies ran while one was open for 3% of the time, Pallas kernels for 0%

commit v1 on v0

v1 whole, which is shorter than its diff:
```python
import functools
import math

import jax
import jax.numpy as jnp
from jax import lax
from jax.experimental import pallas as pl
from jax.experimental.pallas import tpu as pltpu
from jax.sharding import PartitionSpec as P

PATCH_CELLS = 128
RIM = 256
STEPS = 3
NS_ITERS = 6
CHUNKS = 2
F32 = jnp.float32
BF16 = jnp.bfloat16
NN = ((1,), (0,))
NT = ((1,), (1,))
TN = ((0,), (0,))


def dot(a, b, dims=NN):
    return lax.dot_general(a, b, (dims, ((), ())), preferred_element_type=F32)


def halves(a):
    high = a.astype(BF16)
    return high, (a - high.astype(F32)).astype(BF16)


def dot_pair(a, b, dims=NN):
    return dot(a[0], b[0], dims) + (dot(a[0], b[1], dims) + dot(a[1], b[0], dims))


def iota(shape, axis):
    return lax.broadcasted_iota(jnp.int32, shape, axis)


def kernel(
    groups, regions, slots,
    state, adjacent, rates, speed, obs_patch, obs_row, obs_value, obs_error,
    out,
    field, pad, mats, final, ensemble, message, relay, got, result, returned, merged,
    halo_send, halo_recv, first_send, first_recv, second_send, second_recv,
    spread_send, spread_recv, back_send, back_recv,
):
    me = lax.axis_index("member")
    here = lax.axis_index("region")
    right = lax.rem(here + 1, regions)
    left = lax.rem(here + regions - 1, regions)
    members, levels, length = state.shape
    rows = members * levels
    members_all = members * groups
    cells_all = length * regions
    blocks = length // RIM

    barrier = pltpu.get_barrier_semaphore()
    for step in range(1, groups):
        pl.semaphore_signal(barrier, inc=1, device_id={"member": lax.rem(me + step, groups)})
    for step in range(1, regions):
        pl.semaphore_signal(barrier, inc=1, device_id={"region": lax.rem(here + step, regions)})

    for level in range(levels):
        value = state[:, level, :]
        part = pl.ds(level * members, members)
        field[part, :] = value
        pad[0, part, RIM:RIM + length] = value.astype(BF16)

    pl.semaphore_wait(barrier, groups + regions - 2)

    height = rows // CHUNKS

    def halo(step, chunk):
        part = pl.ds(chunk * height, height)
        to_left = pltpu.make_async_remote_copy(
            src_ref=pad.at[step, part, pl.ds(RIM, RIM)],
            dst_ref=pad.at[step, part, pl.ds(RIM + length, RIM)],
            send_sem=halo_send.at[step, chunk, 0],
            recv_sem=halo_recv.at[step, chunk, 1],
            device_id={"region": left},
        )
        to_right = pltpu.make_async_remote_copy(
            src_ref=pad.at[step, part, pl.ds(length, RIM)],
            dst_ref=pad.at[step, part, pl.ds(0, RIM)],
            send_sem=halo_send.at[step, chunk, 1],
            recv_sem=halo_recv.at[step, chunk, 0],
            device_id={"region": right},
        )
        return to_left, to_right

    for chunk in range(CHUNKS):
        for copy in halo(0, chunk):
            copy.start()

    def first(target, source):
        return pltpu.make_async_remote_copy(
            src_ref=message.at[target], dst_ref=relay.at[source],
            send_sem=first_send.at[target], recv_sem=first_recv.at[source],
            device_id={"region": target},
        )

    def second(target, source):
        return pltpu.make_async_remote_copy(
            src_ref=relay.at[:, pl.ds(target * slots, slots), :], dst_ref=got.at[source],
            send_sem=second_send.at[target], recv_sem=second_recv.at[source],
            device_id={"member": target},
        )

    devices = groups * regions
    patch = obs_patch[...]
    count = patch.shape[1]
    live = patch >= 0
    one_hot = (iota((devices, count), 0) == patch).astype(F32)
    upper = (iota((count, count), 0) <= iota((count, count), 1)).astype(F32)
    counts = dot(one_hot.astype(BF16), upper.astype(BF16))
    rank = jnp.sum(counts * one_hot, axis=0, keepdims=True) - 1.0
    spot = jnp.where(live, patch * slots + rank.astype(jnp.int32), -1)
    error = obs_error[...]
    payload = jnp.concatenate(
        [
            (obs_row[...] + 1).astype(F32), obs_value[...], 1.0 / (error * error),
            jnp.zeros((125, count), F32),
        ],
        axis=0,
    )
    place = (iota((devices * slots, count), 0) == spot).astype(F32).astype(BF16)
    high = payload.astype(BF16)
    rest = payload - high.astype(F32)
    middle, low = halves(rest)
    bundle = dot(place, high, NT) + dot(place, middle, NT) + dot(place, low, NT)
    message[...] = bundle.reshape(regions, groups * slots, 128)
    for region in range(regions):
        @pl.when(here != region)
        def _():
            first(region, here).start()
    relay[here] = message[here]

    cell = here * length + iota((1, length), 1)
    offset = adjacent[...] - cell
    offset = jnp.where(offset > cells_all // 2, offset - cells_all, offset)
    offset = jnp.where(offset < -(cells_all // 2), offset + cells_all, offset)
    source = offset + RIM + lax.rem(iota((1, length), 1), RIM)
    rate = rates[...]
    keep = 1.0 - jnp.sum(rate, axis=0, keepdims=True)
    pace = speed[...]
    window = 3 * RIM
    slab = 128
    for block in range(blocks):
        cut = slice(block * RIM, (block + 1) * RIM)
        local, weight = source[:, cut], rate[:, cut]

        def build(index, carry):
            start = pl.multiple_of(index * slab, slab)
            row = iota((slab, RIM), 0) + start
            total = jnp.zeros((slab, RIM), F32)
            for k in range(6):
                total = total + jnp.where(row == local[k:k + 1], weight[k:k + 1], 0.0)
            mats[block, pl.ds(start, slab), :] = total.astype(BF16)
            return carry

        lax.fori_loop(0, window // slab, build, 0)

    for region in range(regions):
        @pl.when(here != region)
        def _():
            first(here, region).wait_recv()
    for member in range(groups):
        @pl.when(me != member)
        def _():
            second(member, me).start()
    got[me] = relay[:, pl.ds(pl.multiple_of(me * slots, slots), slots), :]

    def advance(step, block, start, size):
        part = pl.ds(start, size)
        cut = pl.ds(block * RIM, RIM)
        share = slice(block * RIM, (block + 1) * RIM)
        taken = pad[step, part, block * RIM:block * RIM + window]
        blended = field[part, cut] * keep[:, share] + dot(taken, mats[block])
        new = blended + pace[:, share] * jnp.tanh(blended)
        if step < STEPS - 1:
            field[part, cut] = new
            pad[step + 1, part, pl.ds(RIM + block * RIM, RIM)] = new.astype(BF16)
        else:
            rounded = new.astype(BF16)
            lots = RIM // PATCH_CELLS
            for lot in range(lots):
                piece = rounded[:, lot * PATCH_CELLS:(lot + 1) * PATCH_CELLS]
                final[block * lots + lot, start // members:(start + size) // members] = (
                    piece.reshape(size // members, members, PATCH_CELLS)
                )

    def spread(target, origin):
        return pltpu.make_async_remote_copy(
            src_ref=final.at[target],
            dst_ref=ensemble.at[:, pl.ds(pl.multiple_of(origin * members, members), members), :],
            send_sem=spread_send.at[target], recv_sem=spread_recv.at[origin],
            device_id={"member": target},
        )

    def hand_out(targets):
        for target in targets:
            @pl.when(me != target)
            def _():
                spread(target, me).start()

    lots = RIM // PATCH_CELLS
    for step in range(STEPS):
        for block in range(1, blocks - 1):
            advance(step, block, 0, rows)
        if step == STEPS - 1:
            hand_out(range(lots, groups - lots))
        for chunk in range(CHUNKS):
            _, to_right = halo(step, chunk)
            to_right.wait_recv()
            advance(step, 0, chunk * height, height)
            if step < STEPS - 1:
                halo(step + 1, chunk)[0].start()
            to_left, _ = halo(step, chunk)
            to_left.wait_recv()
            advance(step, blocks - 1, chunk * height, height)
            if step < STEPS - 1:
                halo(step + 1, chunk)[1].start()
    hand_out(list(range(lots)) + list(range(groups - lots, groups)))
    ensemble[:, pl.ds(pl.multiple_of(me * members, members), members), :] = final[me]

    for member in range(groups):
        @pl.when(me != member)
        def _():
            second(me, member).wait_recv()
    span = levels * PATCH_CELLS
    seen = got[...].reshape(devices * slots, 128)
    location = seen[:, 0:1].astype(jnp.int32) - 1
    reading, weight = seen[:, 1:2], seen[:, 2:3]
    select = (iota((devices * slots, span), 1) == location).astype(F32).astype(BF16)
    rooted = jnp.sqrt(weight)
    divisor = math.sqrt(members_all - 1.0)

    for member in range(groups):
        @pl.when(me != member)
        def _():
            spread(me, member).wait_recv()
    whole = jnp.concatenate([ensemble[level] for level in range(levels)], axis=1)
    observed = dot(select, whole, NT)
    average_observed = jnp.sum(observed, axis=1, keepdims=True) * (1.0 / members_all)
    scaled = (observed - average_observed) * (rooted / divisor)
    innovation = rooted * (reading - average_observed)
    forcing = jnp.sum(scaled * innovation, axis=0, keepdims=True) / divisor
    identity = (
        iota((members_all, members_all), 0) == iota((members_all, members_all), 1)
    ).astype(F32)
    parts = halves(scaled)
    system = identity + dot_pair(parts, parts, TN)
    norm = jnp.sqrt(jnp.sum(system * system, keepdims=True))
    iterate = system / norm
    factor = 1.5 * identity - 0.5 * iterate
    factor_parts = halves(factor)
    iterate = dot_pair(halves(iterate), factor_parts)
    inverse = factor
    inverse_parts = factor_parts
    for sweep in range(1, NS_ITERS):
        iterate_parts = halves(iterate)
        factor = 1.5 * identity - 0.5 * dot_pair(inverse_parts, iterate_parts)
        factor_parts = halves(factor)
        if sweep < NS_ITERS - 1:
            iterate = dot_pair(iterate_parts, factor_parts)
        inverse = dot_pair(factor_parts, inverse_parts)
        inverse_parts = halves(inverse)
    inner = jnp.sum(inverse * forcing, axis=1, keepdims=True)
    shift = jnp.sum(inverse * inner, axis=0, keepdims=True) / norm
    transform = halves(inverse / jnp.sqrt(norm) + shift)

    wide = whole.astype(F32)
    average = jnp.sum(wide, axis=0, keepdims=True) * (1.0 / members_all)
    anomaly = halves(wide - average)
    updated = (average + dot_pair(transform, anomaly)).astype(BF16)
    for level in range(levels):
        result[level] = updated[:, level * PATCH_CELLS:(level + 1) * PATCH_CELLS]

    def back(target, origin):
        return pltpu.make_async_remote_copy(
            src_ref=result.at[:, pl.ds(pl.multiple_of(target * members, members), members), :],
            dst_ref=returned.at[origin],
            send_sem=back_send.at[target], recv_sem=back_recv.at[origin],
            device_id={"member": target},
        )

    for target in range(groups):
        @pl.when(me != target)
        def _():
            back(target, me).start()
    returned[me] = result[:, pl.ds(pl.multiple_of(me * members, members), members), :]

    for step in range(STEPS):
        for chunk in range(CHUNKS):
            for copy in halo(step, chunk):
                copy.wait_send()
    for region in range(regions):
        @pl.when(here != region)
        def _():
            first(region, here).wait_send()
    for member in range(groups):
        @pl.when(me != member)
        def _():
            second(member, me).wait_send()
            spread(member, me).wait_send()
            back(me, member).wait_recv()
    for origin in range(groups):
        for level in range(levels):
            merged[:, level, origin * PATCH_CELLS:(origin + 1) * PATCH_CELLS] = (
                returned[origin, level].astype(F32)
            )
    out[...] = merged[...].astype(BF16)
    for member in range(groups):
        @pl.when(me != member)
        def _():
            back(member, me).wait_send()


def on_device(
    state, adjacent_columns, adjacent_rates, amplification_speed,
    obs_patch, obs_row, obs_value, obs_error,
):
    members, levels, length = state.shape
    groups = lax.axis_size("member")
    regions = lax.axis_size("region")
    rows = members * levels
    members_all = members * groups
    count = obs_patch.shape[0]
    slots = -(-count // (groups * regions) // 8) * 8
    dma = pltpu.SemaphoreType.DMA
    vmem = pl.BlockSpec(memory_space=pltpu.VMEM)
    return pl.pallas_call(
        functools.partial(kernel, groups, regions, slots),
        out_shape=jax.ShapeDtypeStruct((members, levels, length), BF16),
        in_specs=[vmem] * 8,
        out_specs=vmem,
        scratch_shapes=[
            pltpu.VMEM((rows, length), F32),
            pltpu.VMEM((STEPS, rows, length + 2 * RIM), BF16),
            pltpu.VMEM((length // RIM, 3 * RIM, RIM), BF16),
            pltpu.VMEM((groups, levels, members, PATCH_CELLS), BF16),
            pltpu.VMEM((levels, members_all, PATCH_CELLS), BF16),
            pltpu.VMEM((regions, groups * slots, 128), F32),
            pltpu.VMEM((regions, groups * slots, 128), F32),
            pltpu.VMEM((groups, regions, slots, 128), F32),
            pltpu.VMEM((levels, members_all, PATCH_CELLS), BF16),
            pltpu.VMEM((groups, levels, members, PATCH_CELLS), BF16),
            pltpu.VMEM((members, levels, length), F32),
            dma((STEPS, CHUNKS, 2)), dma((STEPS, CHUNKS, 2)),
            dma((regions,)), dma((regions,)),
            dma((groups,)), dma((groups,)),
            dma((groups,)), dma((groups,)),
            dma((groups,)), dma((groups,)),
        ],
        compiler_params=pltpu.CompilerParams(
            collective_id=0, has_side_effects=True, vmem_limit_bytes=56 * 1024 * 1024
        ),
    )(
        state, adjacent_columns, adjacent_rates, amplification_speed[None, :],
        obs_patch[None, :], obs_row[None, :], obs_value[None, :], obs_error[None, :],
    )


def solution(mesh):
    return jax.shard_map(
        on_device,
        mesh=mesh,
        in_specs=(
            P("member", None, "region"),
            P(None, "region"),
            P(None, "region"),
            P("region"),
            P(("member", "region")),
            P(("member", "region")),
            P(("member", "region")),
            P(("member", "region")),
        ),
        out_specs=P("member", None, "region"),
        check_vma=False,
    )
```

time: 190 us -> 52 us (0.27); the launches traced: 187 us -> 51.3 us
  Pallas kernels: 0 us -> 49.4 us
  local copies, waits for them, and re-layouts: 47.8 us -> 1.87 us
  waiting for transfers between devices: 34.9 us -> 0 us
  matrix products: 33.5 us -> 0 us
  other arithmetic: 21.3 us -> 0 us
  starting transfers between devices: 20.7 us -> 0 us
  loops' own time: 15.3 us -> 0 us
  blocking collectives: 12.1 us -> 0 us
    pallas_call x0 -> x1, Pallas kernels: none -> 49.4 us  [on_device(): pl.pallas_call(functools.partial(kernel, groups, regions, slots), out_sha...]
    dot_general x52 -> x0, matrix products: 33.5 us -> none  [the longest x24 21.4 us: one_block(): jnp.dot(window, matrix, precision=lax.Precision.HIGHEST)]
    dynamic_slice x48 -> x0, local copies, waits for them, and re-layouts: 32.5 us -> none  [the longest x24 18.4 us: one_block(): speed_block = lax.dynamic_slice_in_dim(amplification_speed, first, block, 0)]
    ppermute x6 -> x0, waiting for transfers between devices: 19.1 us -> none  [the longest x3 14.1 us: padded_2(): before = lax.ppermute(last, axis, up)]
    reduce_sum x25 -> x0, other arithmetic: 17.1 us -> none  [the longest x24 17 us: one_block(): jnp.sum(rate_block, axis=0)[None, :]]
    all_to_all x2 -> x0, waiting for transfers between devices: 15.8 us -> none  [the longest x1 9.22 us: on_device(): lax.all_to_all(rounded, 'member', split_axis=2, concat_axis=0, tiled=True)]
    another operation x3 -> x0, loops' own time: 15.3 us -> none  [advance(): produced = lax.map(one_block, jnp.arange(count_blocks, dtype=jnp.int32))]
    ppermute x6 -> x0, starting transfers between devices: 12.9 us -> none  [the longest x3 9.04 us: padded_2(): after = lax.ppermute(first, axis, down)]
  transfers between devices with their start and end apart: 8 -> 0, of which waited for: 6 -> 0; matrix products, arithmetic and copies ran while one was open for 3% -> 0% of each run, Pallas kernels for 0% -> 0%
where the time goes in v1:
time: 52 us; the launch traced here: 51.3 us
  Pallas kernels  49.4 us (95%)
  local copies, waits for them, and re-layouts  1.87 us (4%)
    pallas_call x1, Pallas kernels, on_device(): pl.pallas_call(functools.partial(kernel, groups, regions, slots), out_sha...  49.4 us
    unnamed x1, local copies, waits for them, and re-layouts  1.87 us

profile of v1, /device:TPU:0, one launch (start us, length us, event | category | flops | bytes accessed | tf_op | source)
XLA Modules:
  0.0 51.3 jit_solution(11018058096318241106)
XLA Ops:
  0.0 49.4 %shard_map.82 = bf16[32,8,1024]{2,1,0:T(8,128)(2,1)} custom-call(f32[32,8,1024]{2,1,0:T(8,128)} %state.1, s32[6,1024]{1,0:T(8,128)} %adjacent.1, f32[6,1024]{1,0:T(8,128)} %rates.1, f32[1,1024]{1,0:T(1,128)} %bitcast.5, s32[1,256]{1,0:T(1,128)} %bitcast.6, s32[1,256]{1,0:T(1,128)} %bitcast.7, f32[1,256]{1,0:T(1,128)} %bitcast.8, f32[1,256]{1,0:T(1,128)} %bitcast.9), custom_call_target="tpu_custom_call" | custom-call | tf_op jit(solution)/shard_map/pallas_call | solution.py:333
  49.4 1.9 %copy.10 = bf16[32,8,1024]{2,1,0:T(8,128)(2,1)} copy(bf16[32,8,1024]{2,1,0:T(8,128)(2,1)} %shard_map.82) | data formatting | bytes 1048576

commit v2 on v1

--- a/solution.py
+++ b/solution.py
@@ -12,7 +12,8 @@
 RIM = 256
 STEPS = 3
 NS_ITERS = 6
-CHUNKS = 2
+CHUNKS = 4
+PARTS = 1
 F32 = jnp.float32
 BF16 = jnp.bfloat16
 NN = ((1,), (0,))
@@ -41,7 +42,7 @@
     groups, regions, slots,
     state, adjacent, rates, speed, obs_patch, obs_row, obs_value, obs_error,
     out,
-    field, pad, mats, final, ensemble, message, relay, got, result, returned, merged,
+    field, pad, mats, final, ensemble, message, relay, dense, got, result, returned, merged,
     halo_send, halo_recv, first_send, first_recv, second_send, second_recv,
     spread_send, spread_recv, back_send, back_recv,
 ):
@@ -61,50 +62,55 @@
     for step in range(1, regions):
         pl.semaphore_signal(barrier, inc=1, device_id={"region": lax.rem(here + step, regions)})
 
-    for level in range(levels):
-        value = state[:, level, :]
-        part = pl.ds(level * members, members)
-        field[part, :] = value
-        pad[0, part, RIM:RIM + length] = value.astype(BF16)
-
+    def load(block):
+        for level in range(levels):
+            value = state[:, level, block * RIM:(block + 1) * RIM]
+            part = pl.ds(level * members, members)
+            field[part, block * RIM:(block + 1) * RIM] = value
+            pad[0, part, (block + 1) * RIM:(block + 2) * RIM] = value.astype(BF16)
+
+    load(0)
+    load(blocks - 1)
     pl.semaphore_wait(barrier, groups + regions - 2)
 
     height = rows // CHUNKS
 
-    def halo(step, chunk):
+    def halo(step, chunk, side):
         part = pl.ds(chunk * height, height)
-        to_left = pltpu.make_async_remote_copy(
-            src_ref=pad.at[step, part, pl.ds(RIM, RIM)],
-            dst_ref=pad.at[step, part, pl.ds(RIM + length, RIM)],
-            send_sem=halo_send.at[step, chunk, 0],
-            recv_sem=halo_recv.at[step, chunk, 1],
-            device_id={"region": left},
-        )
-        to_right = pltpu.make_async_remote_copy(
+        if side == 0:
+            return pltpu.make_async_remote_copy(
+                src_ref=pad.at[step, part, pl.ds(RIM, RIM)],
+                dst_ref=pad.at[step, part, pl.ds(RIM + length, RIM)],
+                send_sem=halo_send.at[step, chunk, 0],
+                recv_sem=halo_recv.at[step, chunk, 1],
+                device_id={"region": left},
+            )
+        return pltpu.make_async_remote_copy(
             src_ref=pad.at[step, part, pl.ds(length, RIM)],
             dst_ref=pad.at[step, part, pl.ds(0, RIM)],
             send_sem=halo_send.at[step, chunk, 1],
             recv_sem=halo_recv.at[step, chunk, 0],
             device_id={"region": right},
         )
-        return to_left, to_right
 
     for chunk in range(CHUNKS):
-        for copy in halo(0, chunk):
-            copy.start()
-
-    def first(target, source):
+        for side in range(2):
+            halo(0, chunk, side).start()
+    for block in range(1, blocks - 1):
+        load(block)
+
+    def first(target, origin):
         return pltpu.make_async_remote_copy(
-            src_ref=message.at[target], dst_ref=relay.at[source],
-            send_sem=first_send.at[target], recv_sem=first_recv.at[source],
+            src_ref=message.at[target], dst_ref=relay.at[origin],
+            send_sem=first_send.at[target], recv_sem=first_recv.at[origin],
+            device_id={"member": target},
+        )
+
+    def second(target, origin):
+        return pltpu.make_async_remote_copy(
+            src_ref=dense.at[target], dst_ref=got.at[origin],
+            send_sem=second_send.at[target], recv_sem=second_recv.at[origin],
             device_id={"region": target},
-        )
-
-    def second(target, source):
-        return pltpu.make_async_remote_copy(
-            src_ref=relay.at[:, pl.ds(target * slots, slots), :], dst_ref=got.at[source],
-            send_sem=second_send.at[target], recv_sem=second_recv.at[source],
-            device_id={"member": target},
         )
 
     devices = groups * regions
@@ -115,7 +121,8 @@
     upper = (iota((count, count), 0) <= iota((count, count), 1)).astype(F32)
     counts = dot(one_hot.astype(BF16), upper.astype(BF16))
     rank = jnp.sum(counts * one_hot, axis=0, keepdims=True) - 1.0
-    spot = jnp.where(live, patch * slots + rank.astype(jnp.int32), -1)
+    desk = lax.rem(patch, groups) * regions + patch // groups
+    spot = jnp.where(live, desk * slots + rank.astype(jnp.int32), -1)
     error = obs_error[...]
     payload = jnp.concatenate(
         [
@@ -129,12 +136,12 @@
     rest = payload - high.astype(F32)
     middle, low = halves(rest)
     bundle = dot(place, high, NT) + dot(place, middle, NT) + dot(place, low, NT)
-    message[...] = bundle.reshape(regions, groups * slots, 128)
-    for region in range(regions):
-        @pl.when(here != region)
-        def _():
-            first(region, here).start()
-    relay[here] = message[here]
+    message[...] = bundle.reshape(groups, regions, slots, 128)
+    for member in range(groups):
+        @pl.when(me != member)
+        def _():
+            first(member, me).start()
+    relay[me] = message[me]
 
     cell = here * length + iota((1, length), 1)
     offset = adjacent[...] - cell
@@ -161,15 +168,22 @@
 
         lax.fori_loop(0, window // slab, build, 0)
 
+    for member in range(groups):
+        @pl.when(me != member)
+        def _():
+            first(me, member).wait_recv()
+    used = groups * slots
+    lanes = dense.shape[2]
+    for region in range(regions):
+        block = relay[:, region].reshape(used, 128)
+        if lanes > used:
+            block = jnp.concatenate([block, jnp.zeros((lanes - used, 128), F32)], axis=0)
+        dense[region] = block.T[:8]
     for region in range(regions):
         @pl.when(here != region)
         def _():
-            first(here, region).wait_recv()
-    for member in range(groups):
-        @pl.when(me != member)
-        def _():
-            second(member, me).start()
-    got[me] = relay[:, pl.ds(pl.multiple_of(me * slots, slots), slots), :]
+            second(region, here).start()
+    got[here] = dense[here]
 
     def advance(step, block, start, size):
         part = pl.ds(start, size)
@@ -190,46 +204,58 @@
                     piece.reshape(size // members, members, PATCH_CELLS)
                 )
 
-    def spread(target, origin):
+    deep = levels // CHUNKS
+
+    def spread(target, origin, chunk):
+        part = pl.ds(chunk * deep, deep)
+        place = pl.ds(pl.multiple_of(origin * members, members), members)
         return pltpu.make_async_remote_copy(
-            src_ref=final.at[target],
-            dst_ref=ensemble.at[:, pl.ds(pl.multiple_of(origin * members, members), members), :],
-            send_sem=spread_send.at[target], recv_sem=spread_recv.at[origin],
+            src_ref=final.at[target, part],
+            dst_ref=ensemble.at[part, place, :],
+            send_sem=spread_send.at[target, chunk], recv_sem=spread_recv.at[origin, chunk],
             device_id={"member": target},
         )
 
-    def hand_out(targets):
+    def hand_out(targets, chunk):
         for target in targets:
             @pl.when(me != target)
             def _():
-                spread(target, me).start()
+                spread(target, me, chunk).start()
 
     lots = RIM // PATCH_CELLS
     for step in range(STEPS):
         for block in range(1, blocks - 1):
             advance(step, block, 0, rows)
         if step == STEPS - 1:
-            hand_out(range(lots, groups - lots))
+            for chunk in range(CHUNKS):
+                hand_out(range(lots, groups - lots), chunk)
         for chunk in range(CHUNKS):
-            _, to_right = halo(step, chunk)
-            to_right.wait_recv()
+            halo(step, chunk, 1).wait_recv()
             advance(step, 0, chunk * height, height)
             if step < STEPS - 1:
-                halo(step + 1, chunk)[0].start()
-            to_left, _ = halo(step, chunk)
-            to_left.wait_recv()
+                halo(step + 1, chunk, 0).start()
+            else:
+                hand_out(range(lots), chunk)
+            halo(step, chunk, 0).wait_recv()
             advance(step, blocks - 1, chunk * height, height)
             if step < STEPS - 1:
-                halo(step + 1, chunk)[1].start()
-    hand_out(list(range(lots)) + list(range(groups - lots, groups)))
+                halo(step + 1, chunk, 1).start()
+            else:
+                hand_out(range(groups - lots, groups), chunk)
     ensemble[:, pl.ds(pl.multiple_of(me * members, members), members), :] = final[me]
 
-    for member in range(groups):
-        @pl.when(me != member)
-        def _():
-            second(me, member).wait_recv()
+    for region in range(regions):
+        @pl.when(here != region)
+        def _():
+            second(here, region).wait_recv()
     span = levels * PATCH_CELLS
-    seen = got[...].reshape(devices * slots, 128)
+    seen = jnp.concatenate(
+        [
+            jnp.concatenate([got[region], jnp.zeros((120, lanes), F32)], axis=0).T[:used]
+            for region in range(regions)
+        ],
+        axis=0,
+    )
     location = seen[:, 0:1].astype(jnp.int32) - 1
     reading, weight = seen[:, 1:2], seen[:, 2:3]
     select = (iota((devices * slots, span), 1) == location).astype(F32).astype(BF16)
@@ -239,7 +265,8 @@
     for member in range(groups):
         @pl.when(me != member)
         def _():
-            spread(me, member).wait_recv()
+            for chunk in range(CHUNKS):
+                spread(me, member, chunk).wait_recv()
     whole = jnp.concatenate([ensemble[level] for level in range(levels)], axis=1)
     observed = dot(select, whole, NT)
     average_observed = jnp.sum(observed, axis=1, keepdims=True) * (1.0 / members_all)
@@ -273,39 +300,47 @@
     wide = whole.astype(F32)
     average = jnp.sum(wide, axis=0, keepdims=True) * (1.0 / members_all)
     anomaly = halves(wide - average)
-    updated = (average + dot_pair(transform, anomaly)).astype(BF16)
-    for level in range(levels):
-        result[level] = updated[:, level * PATCH_CELLS:(level + 1) * PATCH_CELLS]
-
-    def back(target, origin):
+    slim = levels // PARTS
+
+    def back(target, origin, part):
+        depth = pl.ds(part * slim, slim)
+        place = pl.ds(pl.multiple_of(target * members, members), members)
         return pltpu.make_async_remote_copy(
-            src_ref=result.at[:, pl.ds(pl.multiple_of(target * members, members), members), :],
-            dst_ref=returned.at[origin],
-            send_sem=back_send.at[target], recv_sem=back_recv.at[origin],
+            src_ref=result.at[depth, place, :],
+            dst_ref=returned.at[origin, depth],
+            send_sem=back_send.at[target, part], recv_sem=back_recv.at[origin, part],
             device_id={"member": target},
         )
 
-    for target in range(groups):
-        @pl.when(me != target)
-        def _():
-            back(target, me).start()
+    for part in range(PARTS):
+        cut = slice(part * slim * PATCH_CELLS, (part + 1) * slim * PATCH_CELLS)
+        taken = anomaly[0][:, cut], anomaly[1][:, cut]
+        updated = (average[:, cut] + dot_pair(transform, taken)).astype(BF16)
+        for level in range(slim):
+            result[part * slim + level] = updated[:, level * PATCH_CELLS:(level + 1) * PATCH_CELLS]
+        for step in range(1, groups):
+            back(lax.rem(me + step, groups), me, part).start()
     returned[me] = result[:, pl.ds(pl.multiple_of(me * members, members), members), :]
 
     for step in range(STEPS):
         for chunk in range(CHUNKS):
-            for copy in halo(step, chunk):
-                copy.wait_send()
+            for side in range(2):
+                halo(step, chunk, side).wait_send()
     for region in range(regions):
         @pl.when(here != region)
         def _():
-            first(region, here).wait_send()
+            second(region, here).wait_send()
     for member in range(groups):
         @pl.when(me != member)
         def _():
-            second(member, me).wait_send()
-            spread(member, me).wait_send()
-            back(me, member).wait_recv()
+            first(member, me).wait_send()
+            for chunk in range(CHUNKS):
+                spread(member, me, chunk).wait_send()
     for origin in range(groups):
+        @pl.when(me != origin)
+        def _():
+            for part in range(PARTS):
+                back(me, origin, part).wait_recv()
         for level in range(levels):
             merged[:, level, origin * PATCH_CELLS:(origin + 1) * PATCH_CELLS] = (
                 returned[origin, level].astype(F32)
@@ -314,7 +349,8 @@
     for member in range(groups):
         @pl.when(me != member)
         def _():
-            back(member, me).wait_send()
+            for part in range(PARTS):
+                back(member, me, part).wait_send()
 
 
 def on_device(
@@ -341,17 +377,18 @@
             pltpu.VMEM((length // RIM, 3 * RIM, RIM), BF16),
             pltpu.VMEM((groups, levels, members, PATCH_CELLS), BF16),
             pltpu.VMEM((levels, members_all, PATCH_CELLS), BF16),
-            pltpu.VMEM((regions, groups * slots, 128), F32),
-            pltpu.VMEM((regions, groups * slots, 128), F32),
             pltpu.VMEM((groups, regions, slots, 128), F32),
+            pltpu.VMEM((groups, regions, slots, 128), F32),
+            pltpu.VMEM((regions, 8, -(-groups * slots // 128) * 128), F32),
+            pltpu.VMEM((regions, 8, -(-groups * slots // 128) * 128), F32),
             pltpu.VMEM((levels, members_all, PATCH_CELLS), BF16),
             pltpu.VMEM((groups, levels, members, PATCH_CELLS), BF16),
             pltpu.VMEM((members, levels, length), F32),
             dma((STEPS, CHUNKS, 2)), dma((STEPS, CHUNKS, 2)),
+            dma((groups,)), dma((groups,)),
             dma((regions,)), dma((regions,)),
-            dma((groups,)), dma((groups,)),
-            dma((groups,)), dma((groups,)),
-            dma((groups,)), dma((groups,)),
+            dma((groups, CHUNKS)), dma((groups, CHUNKS)),
+            dma((groups, PARTS)), dma((groups, PARTS)),
         ],
         compiler_params=pltpu.CompilerParams(
             collective_id=0, has_side_effects=True, vmem_limit_bytes=56 * 1024 * 1024

time: 52 us -> 46.5 us (0.89)
  Pallas kernels: 49.4 us -> 43.9 us
    pallas_call x1, Pallas kernels: 49.4 us -> 43.9 us  [on_device(): pl.pallas_call(functools.partial(kernel, groups, regions, slots), out_sha...]
where the time goes in v2:
time: 46.5 us; the launch traced here: 45.8 us
  Pallas kernels  43.9 us (94%)
  local copies, waits for them, and re-layouts  1.87 us (4%)
    pallas_call x1, Pallas kernels, on_device(): pl.pallas_call(functools.partial(kernel, groups, regions, slots), out_sha...  43.9 us
    unnamed x1, local copies, waits for them, and re-layouts  1.87 us

profile of v2, /device:TPU:0, one launch (start us, length us, event | category | flops | bytes accessed | tf_op | source)
XLA Modules:
  0.0 45.8 jit_solution(16619168896807953546)
XLA Ops:
  0.0 43.9 %shard_map.82 = bf16[32,8,1024]{2,1,0:T(8,128)(2,1)} custom-call(f32[32,8,1024]{2,1,0:T(8,128)} %state.1, s32[6,1024]{1,0:T(8,128)} %adjacent.1, f32[6,1024]{1,0:T(8,128)} %rates.1, f32[1,1024]{1,0:T(1,128)} %bitcast.5, s32[1,256]{1,0:T(1,128)} %bitcast.6, s32[1,256]{1,0:T(1,128)} %bitcast.7, f32[1,256]{1,0:T(1,128)} %bitcast.8, f32[1,256]{1,0:T(1,128)} %bitcast.9), custom_call_target="tpu_custom_call" | custom-call | tf_op jit(solution)/shard_map/pallas_call | solution.py:369
  43.9 1.9 %copy.10 = bf16[32,8,1024]{2,1,0:T(8,128)(2,1)} copy(bf16[32,8,1024]{2,1,0:T(8,128)(2,1)} %shard_map.82) | data formatting | bytes 1048576

commit v3 on v2

--- a/solution.py
+++ b/solution.py
@@ -44,7 +44,7 @@
     out,
     field, pad, mats, final, ensemble, message, relay, dense, got, result, returned, merged,
     halo_send, halo_recv, first_send, first_recv, second_send, second_recv,
-    spread_send, spread_recv, back_send, back_recv,
+    spread_send, spread_recv, back_send, back_recv, fetched,
 ):
     me = lax.axis_index("member")
     here = lax.axis_index("region")
@@ -62,9 +62,20 @@
     for step in range(1, regions):
         pl.semaphore_signal(barrier, inc=1, device_id={"region": lax.rem(here + step, regions)})
 
+    def fetch(block):
+        cut = pl.ds(block * RIM, RIM)
+        return pltpu.make_async_copy(
+            state.at[:, :, cut], merged.at[:, :, cut], fetched.at[block]
+        )
+
+    inner = list(range(1, blocks - 1))
+    for block in [0, blocks - 1] + inner:
+        fetch(block).start()
+
     def load(block):
+        fetch(block).wait()
         for level in range(levels):
-            value = state[:, level, block * RIM:(block + 1) * RIM]
+            value = merged[:, level, block * RIM:(block + 1) * RIM]
             part = pl.ds(level * members, members)
             field[part, block * RIM:(block + 1) * RIM] = value
             pad[0, part, (block + 1) * RIM:(block + 2) * RIM] = value.astype(BF16)
@@ -96,7 +107,7 @@
     for chunk in range(CHUNKS):
         for side in range(2):
             halo(0, chunk, side).start()
-    for block in range(1, blocks - 1):
+    for block in inner:
         load(block)
 
     def first(target, origin):
@@ -369,7 +380,7 @@
     return pl.pallas_call(
         functools.partial(kernel, groups, regions, slots),
         out_shape=jax.ShapeDtypeStruct((members, levels, length), BF16),
-        in_specs=[vmem] * 8,
+        in_specs=[pl.BlockSpec(memory_space=pl.ANY)] + [vmem] * 7,
         out_specs=vmem,
         scratch_shapes=[
             pltpu.VMEM((rows, length), F32),
@@ -389,6 +400,7 @@
             dma((regions,)), dma((regions,)),
             dma((groups, CHUNKS)), dma((groups, CHUNKS)),
             dma((groups, PARTS)), dma((groups, PARTS)),
+            dma((length // RIM,)),
         ],
         compiler_params=pltpu.CompilerParams(
             collective_id=0, has_side_effects=True, vmem_limit_bytes=56 * 1024 * 1024

time: 46.5 us -> 46.1 us (level)
  no operation moved by 1% of the time
where the time goes in v3:
time: 46.1 us; the launch traced here: 45.4 us
  Pallas kernels  43.5 us (94%)
  local copies, waits for them, and re-layouts  1.87 us (4%)
    pallas_call x1, Pallas kernels, on_device(): pl.pallas_call(functools.partial(kernel, groups, regions, slots), out_sha...  43.5 us
    unnamed x1, local copies, waits for them, and re-layouts  1.87 us

profile of v3, /device:TPU:0, one launch (start us, length us, event | category | flops | bytes accessed | tf_op | source)
XLA Modules:
  0.0 45.4 jit_solution(13221670802884896310)
XLA Ops:
  0.0 43.5 %shard_map.82 = bf16[32,8,1024]{2,1,0:T(8,128)(2,1)} custom-call(f32[32,8,1024]{2,1,0:T(8,128)} %state.1, s32[6,1024]{1,0:T(8,128)} %adjacent.1, f32[6,1024]{1,0:T(8,128)} %rates.1, f32[1,1024]{1,0:T(1,128)} %bitcast.5, s32[1,256]{1,0:T(1,128)} %bitcast.6, s32[1,256]{1,0:T(1,128)} %bitcast.7, f32[1,256]{1,0:T(1,128)} %bitcast.8, f32[1,256]{1,0:T(1,128)} %bitcast.9), custom_call_target="tpu_custom_call" | custom-call | tf_op jit(solution)/shard_map/pallas_call | solution.py:380
  43.5 1.9 %copy.10 = bf16[32,8,1024]{2,1,0:T(8,128)(2,1)} copy(bf16[32,8,1024]{2,1,0:T(8,128)(2,1)} %shard_map.82) | data formatting | bytes 1048576
